TPU v7x, 32 devices: a whole 2x2x4 slice. The times are simulated.
32 devices in a mesh: dp: 4 (over y, x), inner: 8 (over z, core).
Axes of the slice: x: 2, y: 2, z: 4, core: 2. Of those that a mesh axis runs over, the one named last changes fastest.
Arguments:
- queries: bfloat16 [32, 32, 128], P(('dp', 'inner'))
- labels: int32 [32], P(('dp', 'inner')), may hold values from 0 to 127
- pages: bfloat16 [128, 1024, 128], P(('dp', 'inner'))
Outputs:
- grad_queries: float32 [32, 32, 128], P(('dp', 'inner'))
- grad_pages: float32 [128, 1024, 128], P(('dp', 'inner'))
All inputs are finite; a program needn't handle non-finite values.
Results may differ from a plain program's by a relative error of at most 0.0029.
Values may be sent and summed in bfloat16 or wider, within the bound.
No kernel may reach another device: no remote copies, remote signals or barrier semaphores. Data moves between devices by JAX's collectives and lax.ppermute only.
A program may use at most 64 MiB of HBM per device.

v0:
```python
import jax
import jax.numpy as jnp
from jax import lax
from jax.sharding import PartitionSpec as P


def shards(queries, labels, pages):
    pages_here, patch_count, width = pages.shape
    token_count = queries.shape[1]
    first_page = lax.axis_index(("dp", "inner")) * pages_here

    def block_terms(query_block, label_block, page_grads):
        rows_count = query_block.shape[0]
        flat_rows = query_block.reshape(rows_count * token_count, width)
        query_grad = jnp.zeros((rows_count * token_count, width), jnp.float32)
        updated = []
        for page_slot in range(pages_here):
            page_block = pages[page_slot]
            scores = lax.dot_general(
                flat_rows, page_block, (((1,), (1,)), ((), ())), preferred_element_type=jnp.float32
            )
            weights = jax.nn.softmax(scores, axis=-1)
            matched = jnp.sum(weights * scores, axis=-1)
            summed = matched.reshape(rows_count, token_count).sum(axis=1)
            signs = jnp.where(
                label_block == first_page + page_slot, jnp.float32(1.0), jnp.float32(-1.0)
            )
            logits = summed - jnp.float32(token_count)
            grad_score = -signs * jax.nn.sigmoid(-signs * logits)
            row_grad = jnp.broadcast_to(grad_score[:, None], (rows_count, token_count)).reshape(
                rows_count * token_count
            )
            dscore = (row_grad[:, None] * weights * (1.0 + scores - matched[:, None])).astype(
                jnp.bfloat16
            )
            query_grad = query_grad + jnp.dot(
                dscore, page_block, preferred_element_type=jnp.float32
            )
            page_term = lax.dot_general(
                dscore, flat_rows, (((0,), (0,)), ((), ())), preferred_element_type=jnp.float32
            )
            updated.append(page_grads[page_slot] + page_term)
        return (query_grad.reshape(rows_count, token_count, width), jnp.stack(updated))

    empty_pages = jnp.zeros((pages_here, patch_count, width), jnp.float32)
    every_query, every_label = (
        lax.all_gather(queries, ("dp", "inner"), axis=0, tiled=True),
        lax.all_gather(labels, ("dp", "inner"), axis=0, tiled=True),
    )
    page_grads = empty_pages
    rows_count = every_query.shape[0]
    query_blocks = every_query.reshape(rows_count // 16, 16, token_count, width)
    label_blocks = every_label.reshape(rows_count // 16, 16)

    def advance(page_carry, inputs):
        block_grad, page_carry = block_terms(inputs[0], inputs[1], page_carry)
        return (page_carry, block_grad)

    page_grads, block_grads = lax.scan(advance, page_grads, (query_blocks, label_blocks))
    grad_buffer = block_grads.reshape(rows_count, token_count, width)
    partial_sum = lax.psum_scatter(
        grad_buffer.astype(jnp.bfloat16), "dp", scatter_dimension=0, tiled=True
    ).astype(jnp.float32)
    grad_queries = lax.psum_scatter(partial_sum, "inner", scatter_dimension=0, tiled=True)
    return (grad_queries, page_grads)


def solution(mesh):
    placed = (P(("dp", "inner"), None, None), P(("dp", "inner")), P(("dp", "inner"), None, None))
    return jax.shard_map(
        shards,
        mesh=mesh,
        in_specs=placed,
        out_specs=(P(("dp", "inner"), None, None), P(("dp", "inner"), None, None)),
        check_vma=False,
    )
```

profile of v0, /device:TPU:0, one launch (start us, length us, event | category | flops | bytes accessed | tf_op | source)
XLA Modules:
  0.0 223.1 jit_solution(10414008605873370452)
XLA Ops:
  8.1 42.0 %all-reduce = s32[32]{0:T(128)S(1)} all-reduce(s32[32]{0:T(128)S(1)} %dynamic-update-slice), channel_id=1, replica_groups=mesh['dp'=4,'inner'=8] {'dp','inner'}, use_global_device_ids=true, to_apply=%add | all-reduce | flops 32 | bytes 256
  50.1 41.4 %all_gather.7 = bf16[32,32,128]{2,1,0:T(8,128)(2,1)S(1)} all-gather(bf16[1,32,128]{2,1,0:T(8,128)(2,1)} %param.5), channel_id=1, replica_groups=mesh['dp'=4,'inner'=8] {'dp','inner'}, dimensions={0}, use_global_device_ids=true | all-gather | bytes 270336 | tf_op jit(solution)/shard_map/all_gather | solution.py:47
  91.6 1.5 broadcast_in_dim.86
  93.0 68.0 %while.15 = (s32[]{:T(128)}, f32[4,1024,128]{2,1,0:T(8,128)}, bf16[2,16,32,128]{3,2,1,0:T(8,128)(2,1)}, s32[2,16]{1,0:T(2,128)S(1)}, s32[]{:T(128)}, /*index=5*/...) while((s32[]{:T(128)}, f32[4,1024,128]{2,1,0:T(8,128)}, ...), condition=%wide.region_17.18_spmd, body=%wide.region_0.17_spmd.sunk | while | flops 1642328576 | bytes 108293800 | solution.py:59
  94.1 0.8 copy-done
  99.6 0.8 copy-done.2
  101.9 2.3 %multiply_convert_fusion.11 = bf16[512,1024]{1,0:T(8,128)(2,1)S(1)} fusion(f32[512,1024]{1,0:T(8,128)} %copy-done.2, f32[512]{0:T(512)S(1)} %multiply_reduce_fusion.9, f32[512]{0:T(512)S(1)} %mul.311, f32[512]{0:T(512)S(1)} %fusion.117, f32[512]{0:T(512)S(1)} %get-tuple-element.248), kind=kLoop, calls=%fused_computation.10.clone.1 | loop fusion | flops 3670016 | bytes 3153920 | tf_op jit(solution)/shard_map/while/body/eval_jaxpr/convert_element_type | solution.py:33
  104.6 2.3 %fusion.125 = f32[1,1024,128]{2,1,0:T(8,128)} fusion(bf16[512,1024]{1,0:T(8,128)(2,1)S(1)} %multiply_convert_fusion.11, bf16[512,128]{1,0:T(8,128)(2,1)S(1)} %bitcast.155, f32[4,1024,128]{2,1,0:T(8,128)} %get-tuple-element.271), kind=kOutput, calls=%fused_computation.25.clone.1 | convolution fusion | flops 134348800 | bytes 2228224 | tf_op jit(solution)/shard_map/while/body/eval_jaxpr/dot_general | solution.py:39
  108.0 0.8 copy-done.1
  110.3 3.2 %multiply_convert_fusion.8 = bf16[512,1024]{1,0:T(8,128)(2,1)} fusion(f32[512,1024]{1,0:T(8,128)} %copy-done.1, f32[512]{0:T(512)S(1)} %multiply_reduce_fusion.8, f32[512]{0:T(512)S(1)} %mul.308, f32[512]{0:T(512)S(1)} %fusion.115, f32[512]{0:T(512)S(1)} %get-tuple-element.246), kind=kLoop, calls=%fused_computation.1.clone.1 | loop fusion | flops 3670016 | bytes 3153920 | tf_op jit(solution)/shard_map/while/body/eval_jaxpr/convert_element_type | solution.py:33
  113.7 2.3 %multiply_convert_fusion.9 = bf16[512,1024]{1,0:T(8,128)(2,1)S(1)} fusion(f32[512,1024]{1,0:T(8,128)} %copy-done, f32[512]{0:T(512)} %copy-done.10, f32[512]{0:T(512)S(1)} %mul.309, f32[512]{0:T(512)} %copy-done.12, f32[512]{0:T(512)S(1)} %get-tuple-element.253), kind=kLoop, calls=%fused_computation.4.clone.1 | loop fusion | flops 3670016 | bytes 3153920 | tf_op jit(solution)/shard_map/while/body/eval_jaxpr/convert_element_type | solution.py:33
  117.3 1.5 multiply_convert_fusion.10
  118.8 1.4 convolution_add_fusion.10
  120.7 1.5 convolution_add_fusion.11
  122.7 1.4 convolution_add_fusion.12
  124.7 1.6 pad_maximum_fusion.2
  126.3 0.7 copy-done.14
  128.1 0.8 copy-done
  133.6 0.8 copy-done.2
  135.9 2.3 %multiply_convert_fusion.11 = bf16[512,1024]{1,0:T(8,128)(2,1)S(1)} fusion(f32[512,1024]{1,0:T(8,128)} %copy-done.2, f32[512]{0:T(512)S(1)} %multiply_reduce_fusion.9, f32[512]{0:T(512)S(1)} %mul.311, f32[512]{0:T(512)S(1)} %fusion.117, f32[512]{0:T(512)S(1)} %get-tuple-element.248), kind=kLoop, calls=%fused_computation.10.clone.1 | loop fusion | flops 3670016 | bytes 3153920 | tf_op jit(solution)/shard_map/while/body/eval_jaxpr/convert_element_type | solution.py:33
  138.6 2.3 %fusion.125 = f32[1,1024,128]{2,1,0:T(8,128)} fusion(bf16[512,1024]{1,0:T(8,128)(2,1)S(1)} %multiply_convert_fusion.11, bf16[512,128]{1,0:T(8,128)(2,1)S(1)} %bitcast.155, f32[4,1024,128]{2,1,0:T(8,128)} %get-tuple-element.271), kind=kOutput, calls=%fused_computation.25.clone.1 | convolution fusion | flops 134348800 | bytes 2228224 | tf_op jit(solution)/shard_map/while/body/eval_jaxpr/dot_general | solution.py:39
  142.0 0.8 copy-done.1
  144.3 3.2 %multiply_convert_fusion.8 = bf16[512,1024]{1,0:T(8,128)(2,1)} fusion(f32[512,1024]{1,0:T(8,128)} %copy-done.1, f32[512]{0:T(512)S(1)} %multiply_reduce_fusion.8, f32[512]{0:T(512)S(1)} %mul.308, f32[512]{0:T(512)S(1)} %fusion.115, f32[512]{0:T(512)S(1)} %get-tuple-element.246), kind=kLoop, calls=%fused_computation.1.clone.1 | loop fusion | flops 3670016 | bytes 3153920 | tf_op jit(solution)/shard_map/while/body/eval_jaxpr/convert_element_type | solution.py:33
  147.7 2.3 %multiply_convert_fusion.9 = bf16[512,1024]{1,0:T(8,128)(2,1)S(1)} fusion(f32[512,1024]{1,0:T(8,128)} %copy-done, f32[512]{0:T(512)} %copy-done.10, f32[512]{0:T(512)S(1)} %mul.309, f32[512]{0:T(512)} %copy-done.12, f32[512]{0:T(512)S(1)} %get-tuple-element.253), kind=kLoop, calls=%fused_computation.4.clone.1 | loop fusion | flops 3670016 | bytes 3153920 | tf_op jit(solution)/shard_map/while/body/eval_jaxpr/convert_element_type | solution.py:33
  151.3 1.5 multiply_convert_fusion.10
  152.8 1.4 convolution_add_fusion.10
  154.7 1.5 convolution_add_fusion.11
  156.7 1.4 convolution_add_fusion.12
  158.7 1.6 pad_maximum_fusion.2
  161.1 21.7 %reduce-scatter.3.cloned.1.call-done = bf16[8,32,128]{2,1,0:T(8,128)(2,1)} async-done(((bf16[32,32,128]{2,1,0:T(8,128)(2,1)}), bf16[8,32,128]{2,1,0:T(8,128)(2,1)}) %reduce-scatter.3.cloned.1.call-update) | async-done | bytes 65552 | tf_op jit(solution)/shard_map/reduce_scatter | solution.py:61
  182.8 1.5 convert_element_type.39
  184.3 31.9 %reduce-scatter.5.cloned.1.call-done = f32[1,32,128]{2,1,0:T(8,128)} async-done(((f32[8,32,128]{2,1,0:T(8,128)}), f32[1,32,128]{2,1,0:T(8,128)}) %reduce-scatter.5.cloned.1.call-update) | async-done | bytes 16400 | tf_op jit(solution)/shard_map/reduce_scatter | solution.py:64
  (151 shorter events, 27.4 us)
Async XLA Ops:
  7.2 85.8 %copy-start.4 = (bf16[4,1024,128]{2,1,0:T(8,128)(2,1)S(1)}, bf16[4,1024,128]{2,1,0:T(8,128)(2,1)}, u32[]{:S(2)}) copy-start(bf16[4,1024,128]{2,1,0:T(8,128)(2,1)} %param.7) | copy-start | bytes 3145732
  7.2 175.6 %reduce-scatter.3.cloned.1.call-start = ((), (), s32[]{:S(2)}) async-start(), calls=%async_computation.2 | async-start | bytes 327680 | tf_op jit(solution)/shard_map/reduce_scatter | solution.py:61
  93.0 8.2 %copy-start.18 = (s32[2,16]{1,0:T(2,128)}, s32[2,16]{1,0:T(2,128)S(1)}, u32[]{:S(2)}) copy-start(s32[2,16]{1,0:T(2,128)S(1)} %get-tuple-element.285) | copy-start | bytes 388 | tf_op jit(solution)/shard_map/while
  93.5 1.4 copy-start
  94.9 1.8 copy-start.12
  95.5 1.7 copy-start.10
  99.1 1.3 copy-start.2
  107.5 2.1 copy-start.15
  107.5 2.1 copy-start.16
  107.5 2.1 copy-start.17
  117.3 2.9 %copy-start.6 = (f32[4,1024,128]{2,1,0:T(8,128)S(1)}, f32[4,1024,128]{2,1,0:T(8,128)}, u32[]{:S(2)}) copy-start(f32[4,1024,128]{2,1,0:T(8,128)} %get-tuple-element.271) | copy-start | bytes 6291460 | tf_op jit(solution)/shard_map/while
  120.7 2.0 copy-start.3
  122.7 1.9 copy-start.7
  124.6 1.6 copy-start.13
  124.7 2.3 %copy-start.5 = (bf16[4,1024,128]{2,1,0:T(8,128)(2,1)S(1)}, bf16[4,1024,128]{2,1,0:T(8,128)(2,1)}, u32[]{:S(2)}) copy-start(bf16[4,1024,128]{2,1,0:T(8,128)(2,1)} %get-tuple-element.308) | copy-start | bytes 3145732 | tf_op jit(solution)/shard_map/while
  124.7 2.3 %copy-start.9 = (bf16[2,16,32,128]{3,2,1,0:T(8,128)(2,1)S(1)}, bf16[2,16,32,128]{3,2,1,0:T(8,128)(2,1)}, u32[]{:S(2)}) copy-start(bf16[2,16,32,128]{3,2,1,0:T(8,128)(2,1)} %copy-done.8) | copy-start | bytes 786436 | tf_op jit(solution)/shard_map/while
  124.7 2.3 %copy-start.19 = (s32[2,16]{1,0:T(2,128)S(1)}, s32[2,16]{1,0:T(2,128)}, u32[]{:S(2)}) copy-start(s32[2,16]{1,0:T(2,128)} %copy-done.18) | copy-start | bytes 388 | tf_op jit(solution)/shard_map/while
  127.0 8.2 %copy-start.18 = (s32[2,16]{1,0:T(2,128)}, s32[2,16]{1,0:T(2,128)S(1)}, u32[]{:S(2)}) copy-start(s32[2,16]{1,0:T(2,128)S(1)} %get-tuple-element.285) | copy-start | bytes 388 | tf_op jit(solution)/shard_map/while
  127.5 1.4 copy-start
  128.9 1.8 copy-start.12
  129.5 1.7 copy-start.10
  141.5 2.1 copy-start.15
  141.5 2.1 copy-start.16
  141.5 2.1 copy-start.17
  151.3 2.9 %copy-start.6 = (f32[4,1024,128]{2,1,0:T(8,128)S(1)}, f32[4,1024,128]{2,1,0:T(8,128)}, u32[]{:S(2)}) copy-start(f32[4,1024,128]{2,1,0:T(8,128)} %get-tuple-element.271) | copy-start | bytes 6291460 | tf_op jit(solution)/shard_map/while
  154.7 2.0 copy-start.3
  156.7 1.9 copy-start.7
  158.6 1.6 copy-start.13
  158.7 2.3 %copy-start.5 = (bf16[4,1024,128]{2,1,0:T(8,128)(2,1)S(1)}, bf16[4,1024,128]{2,1,0:T(8,128)(2,1)}, u32[]{:S(2)}) copy-start(bf16[4,1024,128]{2,1,0:T(8,128)(2,1)} %get-tuple-element.308) | copy-start | bytes 3145732 | tf_op jit(solution)/shard_map/while
  158.7 2.3 %copy-start.9 = (bf16[2,16,32,128]{3,2,1,0:T(8,128)(2,1)S(1)}, bf16[2,16,32,128]{3,2,1,0:T(8,128)(2,1)}, u32[]{:S(2)}) copy-start(bf16[2,16,32,128]{3,2,1,0:T(8,128)(2,1)} %copy-done.8) | copy-start | bytes 786436 | tf_op jit(solution)/shard_map/while
  158.7 2.3 %copy-start.19 = (s32[2,16]{1,0:T(2,128)S(1)}, s32[2,16]{1,0:T(2,128)}, u32[]{:S(2)}) copy-start(s32[2,16]{1,0:T(2,128)} %copy-done.18) | copy-start | bytes 388 | tf_op jit(solution)/shard_map/while
  161.0 55.2 %reduce-scatter.5.cloned.1.call-start = ((), (), s32[]{:S(2)}) async-start(), calls=%async_computation.3 | async-start | bytes 147456 | tf_op jit(solution)/shard_map/reduce_scatter | solution.py:64
  (9 other events, 8.8 us)
Sparse Core Ops, SparseCore 0:
  161.1 21.6 reduce-scatter.2
  185.6 30.5 reduce-scatter.4
where the time goes:
time: 224 us; the launch traced here: 223 us
  blocking collectives  83.4 us (37%)
  waiting for transfers between devices  53.7 us (24%)
  other arithmetic  37.3 us (17%)
  matrix products  21.1 us (9%)
  between operations  14.8 us (7%)
  local copies, waits for them, and re-layouts  12.2 us (5%)
    unnamed x1, blocking collectives  42 us
    all_gather x1, blocking collectives, shards(): lax.all_gather(queries, ('dp', 'inner'), axis=0, tiled=True)  41.4 us
    reduce_scatter x1, waiting for transfers between devices, shards(): lax.psum_scatter(partial_sum, 'inner', scatter_dimension=0, tiled=True)  31.9 us
    reduce_scatter x1, waiting for transfers between devices, shards(): lax.psum_scatter(grad_buffer.astype(jnp.bfloat16), 'dp', scatter_dimensio...  21.7 us
    convert_element_type x8, other arithmetic, block_terms(): (row_grad[:, None] * weights * (1.0 + scores - matched[:, None])).astype(...  18.5 us
    dot_general x8, matrix products, block_terms(): jnp.dot(dscore, page_block, preferred_element_type=jnp.float32)  9.52 us
    dot_general x8, matrix products, block_terms(): lax.dot_general(dscore, flat_rows, (((0,), (0,)), ((), ())), preferred_el...  7.48 us
    while x76, local copies, waits for them, and re-layouts  6.3 us
  transfers between devices with their start and end apart: 2, of which 2 were waited for; matrix products, arithmetic and copies ran while one was open for 0% of the time, Pallas kernels for 0%

commit v1 on v0

v1 whole, which is shorter than its diff:
```python
import functools, math
import jax, jax.numpy as jnp
from jax import lax
from jax.experimental import pallas as pl
from jax.experimental.pallas import tpu as pltpu
from jax.sharding import PartitionSpec as P

LOG2E = math.log2(math.e)
LN2 = math.log(2.0)
F32, BF16 = jnp.float32, jnp.bfloat16


def dot(a, b, ca, cb):
    return lax.dot_general(a, b, (((ca,), (cb,)), ((), ())), preferred_element_type=F32)


def split3(x):
    hi = x.astype(BF16)
    r = x - hi.astype(F32)
    mid = r.astype(BF16)
    lo = (r - mid.astype(F32)).astype(BF16)
    return hi, mid, lo


def kernel(tq, tokens, ch, first_ref, qx_ref, pages_ref, gq_ref, gp_hbm,
           qhl, lab, pt, st0, et0, et1, ft0, ft1, mx, stat0, stat1, cs0, cs1, qs0, qs1, gqt, gp, sem):
    npages, lp, d = pages_ref.shape
    nt = qx_ref.shape[0] // tq
    rows = tq * tokens
    n = npages * nt
    nch = lp // ch

    lane_q = lax.broadcasted_iota(jnp.int32, (rows, rows), 1) // tokens
    sub_q = lax.broadcasted_iota(jnp.int32, (rows, rows), 0) // tokens
    seg = (lane_q == sub_q).astype(BF16)

    def setup(t, _):
        blk = qx_ref[pl.ds(t * tq, tq)]
        q = blk[:, :tokens, :].reshape(rows, d)
        qs = q.astype(F32) * LOG2E
        hi = qs.astype(BF16)
        lo = (qs - hi.astype(F32)).astype(BF16)
        qhl[t, :, :d] = hi
        qhl[t, :, d:] = lo
        lrow = blk[:, tokens:tokens + 1, :].reshape(tq, d)
        lane = lax.broadcasted_iota(jnp.int32, (tq, rows), 1) // tokens
        sub = lax.broadcasted_iota(jnp.int32, (tq, rows), 0)
        onehot = (lane == sub).astype(BF16)
        digits = dot(lrow, onehot, 0, 0)
        lab[t] = digits[:8]
        gqt[t] = jnp.zeros((d, rows), F32)
        return 0

    lax.fori_loop(0, nt, setup, 0)

    def setup_p(p, _):
        pt[p] = pages_ref[p].T
        return 0

    lax.fori_loop(0, npages, setup_p, 0)

    def a1(i, c, st):
        p, t = i // nt, i % nt
        q2 = qhl[t]
        sl = slice(c * ch, (c + 1) * ch)
        pc = pages_ref[p, sl, :]
        s = dot(jnp.concatenate([pc, pc], axis=1), q2, 1, 1)
        st[sl, :] = s
        return jnp.max(s.reshape(ch // 8, 8, rows), axis=0)

    def a2(c, m, st, et, ft):
        sl = slice(c * ch, (c + 1) * ch)
        tt = st[sl, :] - m
        e = jnp.exp2(tt)
        f = e * tt
        et[sl, :] = e
        ft[sl, :] = f
        return jnp.sum(e.reshape(ch // 8, 8, rows), axis=0), jnp.sum(f.reshape(ch // 8, 8, rows), axis=0)

    def b0(i, stat):
        p, t = i // nt, i % nt
        m, l, f = stat[0:1], stat[1:2], stat[2:3]
        inv = 1.0 / l
        mm = f * inv
        matched = (mm + m) * LN2
        hi, mid, lo = split3(matched)
        parts = jnp.concatenate([hi.astype(F32), mid.astype(F32), lo.astype(F32), jnp.zeros((5, rows), F32)], axis=0)
        sums = dot(parts.astype(BF16), seg, 1, 0)
        score = sums[0:1] + sums[1:2] + sums[2:3]
        digits = lab[t]
        label = digits[0:1].astype(jnp.int32) * 256 + digits[1:2].astype(jnp.int32)
        sign = jnp.where(label == first_ref[0] + p, 1.0, -1.0).astype(F32)
        logit = score - float(tokens)
        g = -sign * jax.nn.sigmoid(-sign * logit)
        c2 = g * (inv * LN2)
        c1 = LOG2E - mm
        c2col = jnp.broadcast_to(c2, (d, rows)).T
        q = qx_ref[pl.ds(t * tq, tq)][:, :tokens, :].reshape(rows, d)
        qs = (q.astype(F32) * c2col).astype(BF16)
        return c1, c2, qs

    def b1(i, c, c1, qsr, et, ft):
        p = i // nt
        sl = slice(c * ch, (c + 1) * ch)
        ds = (ft[sl, :] + c1 * et[sl, :]).astype(BF16)
        gp[p, sl, :] = gp[p, sl, :] + dot(ds, qsr[...], 1, 0)
        return dot(pt[p, :, sl], ds, 1, 0)

    ets, fts, stats, cs, qss = (et0, et1), (ft0, ft1), (stat0, stat1), (cs0, cs1), (qs0, qs1)

    def step(k, par, w1, w2, w3, w4):
        et, ft = ets[par], fts[par]
        if w4:
            c1, c2 = cs[par][0:1], cs[par][1:2]
        if w2:
            m = jnp.max(mx[...], axis=0, keepdims=True)
        l8 = f8 = m8 = acc = None
        for c in range(nch):
            if w4:
                x = b1(k, c, c1, qss[par], et, ft)
                acc = x if acc is None else acc + x
            if w2:
                le, fe = a2(c, m, st0, et, ft)
                l8, f8 = (le, fe) if l8 is None else (l8 + le, f8 + fe)
            if w1:
                x = a1(k + 3, c, st0)
                m8 = x if m8 is None else jnp.maximum(m8, x)
            if c == 0 and w3:
                c1n, c2n, qsn = b0(k + 1, stats[1 - par])
                cs[1 - par][0:1] = c1n
                cs[1 - par][1:2] = c2n
                qss[1 - par][...] = qsn
        if w1:
            mx[...] = m8
        if w2:
            stats[par][0:1] = m
            stats[par][1:2] = jnp.sum(l8, axis=0, keepdims=True)
            stats[par][2:3] = jnp.sum(f8, axis=0, keepdims=True)
        if w4:
            p, t = k // nt, k % nt
            gqt[t] = gqt[t] + acc * c2
            @pl.when(t == nt - 1)
            def _():
                pltpu.make_async_copy(gp.at[p], gp_hbm.at[p], sem).start()

    for p in range(npages):
        gp[p] = jnp.zeros((lp, d), F32)

    assert n % 2 == 0 and n >= 4
    step(-3, 1, 1, 0, 0, 0)
    step(-2, 0, 1, 1, 0, 0)
    step(-1, 1, 1, 1, 1, 0)

    def body(k, _):
        step(2 * k, 0, 1, 1, 1, 1)
        step(2 * k + 1, 1, 1, 1, 1, 1)
        return 0

    lax.fori_loop(0, n // 2 - 2, body, 0)
    step(n - 4, 0, 1, 1, 1, 1)
    step(n - 3, 1, 0, 1, 1, 1)
    step(n - 2, 0, 0, 0, 1, 1)
    step(n - 1, 1, 0, 0, 0, 1)

    def fin(t, _):
        gq_ref[pl.ds(t * tq, tq)] = gqt[t].T.astype(gq_ref.dtype).reshape(tq, tokens, d)
        return 0
    lax.fori_loop(0, nt, fin, 0)
    for p in range(npages):
        pltpu.make_async_copy(gp.at[p], gp_hbm.at[p], sem).wait()


def call(first, qx, pages, tokens, tq=8, ch=256):
    nq = qx.shape[0]
    npages, lp, d = pages.shape
    rows = tq * tokens
    nt = nq // tq
    return pl.pallas_call(
        functools.partial(kernel, tq, tokens, ch),
        out_shape=(jax.ShapeDtypeStruct((nq, tokens, d), BF16), jax.ShapeDtypeStruct((npages, lp, d), F32)),
        in_specs=[pl.BlockSpec(memory_space=pltpu.SMEM), pl.BlockSpec(memory_space=pltpu.VMEM), pl.BlockSpec(memory_space=pltpu.VMEM)],
        out_specs=(pl.BlockSpec(memory_space=pltpu.VMEM), pl.BlockSpec(memory_space=pl.ANY)),
        scratch_shapes=[
            pltpu.VMEM((nt, rows, 2 * d), BF16),
            pltpu.VMEM((nt, 8, rows), F32),
            pltpu.VMEM((npages, d, lp), BF16),
            pltpu.VMEM((lp, rows), F32),
            pltpu.VMEM((lp, rows), F32),
            pltpu.VMEM((lp, rows), F32),
            pltpu.VMEM((lp, rows), F32),
            pltpu.VMEM((lp, rows), F32),
            pltpu.VMEM((8, rows), F32),
            pltpu.VMEM((8, rows), F32),
            pltpu.VMEM((8, rows), F32),
            pltpu.VMEM((8, rows), F32),
            pltpu.VMEM((8, rows), F32),
            pltpu.VMEM((rows, d), BF16),
            pltpu.VMEM((rows, d), BF16),
            pltpu.VMEM((nt, d, rows), F32),
            pltpu.VMEM((npages, lp, d), F32),
            pltpu.SemaphoreType.DMA,
        ],
        compiler_params=pltpu.CompilerParams(vmem_limit_bytes=40 * 2**20),
        name="pairs",
    )(first, qx, pages)


def shards(queries, labels, pages):
    count, tokens, width = queries.shape
    axes = ("dp", "inner")
    devices = lax.axis_size("dp") * lax.axis_size("inner")
    first = (lax.axis_index(axes) * pages.shape[0]).astype(jnp.int32).reshape(1)
    lane = lax.broadcasted_iota(jnp.int32, (count, 8, width), 2)
    digits = jnp.where(lane == 0, labels[:, None, None] // 256, labels[:, None, None] % 256)
    packed = jnp.concatenate([queries, digits.astype(BF16)], axis=1)
    spread = jnp.broadcast_to(packed[None], (devices,) + packed.shape)
    every = lax.all_to_all(spread, axes, 0, 0, tiled=True).reshape((devices * count,) + packed.shape[1:])
    partial, page_grads = call(first, every, pages, tokens)
    mine = lax.all_to_all(partial.reshape(devices, count, tokens, width), axes, 0, 0, tiled=True)
    return jnp.sum(mine.astype(F32), axis=0), page_grads


def solution(mesh):
    placed = (P(("dp", "inner"), None, None), P(("dp", "inner")), P(("dp", "inner"), None, None))
    return jax.shard_map(
        shards,
        mesh=mesh,
        in_specs=placed,
        out_specs=(P(("dp", "inner"), None, None), P(("dp", "inner"), None, None)),
        check_vma=False,
    )
```

time: 224 us -> 48 us (0.21)
  blocking collectives: 83.4 us -> 12.1 us
  waiting for transfers between devices: 53.7 us -> 12 us
  other arithmetic: 37.3 us -> 1.36 us
  matrix products: 21.1 us -> 0 us
  between operations: 14.8 us -> 1.34 us
  Pallas kernels: 0 us -> 11.3 us
  local copies, waits for them, and re-layouts: 12.2 us -> 2 us
  starting transfers between devices: 0.08 us -> 7.33 us
    reduce_scatter x2 -> x0, waiting for transfers between devices: 53.6 us -> none  [the longest x1 31.9 us: shards(): lax.psum_scatter(partial_sum, 'inner', scatter_dimension=0, tiled=True)]
    unnamed x1 -> x0, blocking collectives: 42 us -> none
    all_gather x1 -> x0, blocking collectives: 41.4 us -> none  [shards(): lax.all_gather(queries, ('dp', 'inner'), axis=0, tiled=True)]
    dot_general x24 -> x0, matrix products: 21.1 us -> none  [the longest x8 9.52 us: block_terms(): jnp.dot(dscore, page_block, preferred_element_type=jnp.float32)]
    convert_element_type x9 -> x1, other arithmetic: 20 us -> 0.01 us  [shards(): packed = jnp.concatenate([queries, digits.astype(BF16)], axis=1)]
    all_to_all x0 -> x1, blocking collectives: none -> 12.1 us  [shards(): lax.all_to_all(partial.reshape(devices, count, tokens, width), axes, 0, 0...]
    all_to_all x0 -> x1, waiting for transfers between devices: none -> 12 us  [shards(): lax.all_to_all(spread, axes, 0, 0, tiled=True)]
    pallas_call x0 -> x1, Pallas kernels: none -> 11.3 us  [call(): pl.pallas_call(functools.partial(kernel, tq, tokens, ch), out_shape=(jax....]
  transfers between devices with their start and end apart: 2 -> 1, of which waited for: 2 -> 1; matrix products, arithmetic and copies ran while one was open for 0% -> 0% of each run, Pallas kernels for 0% -> 0%
where the time goes in v1:
time: 48 us; the launch traced here: 47.4 us
  blocking collectives  12.1 us (25%)
  waiting for transfers between devices  12 us (25%)
  Pallas kernels  11.3 us (24%)
  starting transfers between devices  7.33 us (15%)
  local copies, waits for them, and re-layouts  2 us (4%)
  other arithmetic  1.36 us (3%)
  between operations  1.34 us (3%)
    all_to_all x1, blocking collectives, shards(): lax.all_to_all(partial.reshape(devices, count, tokens, width), axes, 0, 0...  12.1 us
    all_to_all x1, waiting for transfers between devices, shards(): lax.all_to_all(spread, axes, 0, 0, tiled=True)  12 us
    pallas_call x1, Pallas kernels, call(): pl.pallas_call(functools.partial(kernel, tq, tokens, ch), out_shape=(jax....  11.3 us
    all_to_all x1, starting transfers between devices, shards(): lax.all_to_all(spread, axes, 0, 0, tiled=True)  7.33 us
    unnamed x2, local copies, waits for them, and re-layouts  1.22 us
  transfers between devices with their start and end apart: 1, of which 1 were waited for; matrix products, arithmetic and copies ran while one was open for 0% of the time, Pallas kernels for 0%

profile of v1, /device:TPU:0, one launch (start us, length us, event | category | flops | bytes accessed | tf_op | source)
XLA Modules:
  0.0 47.4 jit_solution(9791496349954746886)
XLA Ops:
  1.3 0.7 %maximum_bitcast_fusion = bf16[40,128]{1,0:T(8,128)(2,1)S(1)} fusion(bf16[1,8,128]{2,1,0:T(8,128)(2,1)S(1)} %iota.7, bf16[1,32,128]{2,1,0:T(8,128)(2,1)} %param.3), kind=kLoop, calls=%fused_computation.1 | loop fusion | flops 20480 | bytes 20480 | tf_op jit(solution)/shard_map/broadcast_in_dim | solution.py:216
  2.0 0.8 %broadcast_in_dim.38 = bf16[32,1,40,128]{3,2,1,0:T(8,128)(2,1)} broadcast(bf16[40,128]{1,0:T(8,128)(2,1)S(1)} %maximum_bitcast_fusion), dimensions={2,3} | broadcast | bytes 337920 | tf_op jit(solution)/shard_map/broadcast_in_dim | solution.py:216
  2.8 7.3 %all-to-all-start = ((bf16[32,1,40,128]{3,2,1,0:T(8,128)(2,1)}), bf16[32,1,40,128]{3,2,1,0:T(8,128)(2,1)S(1)}, u32[]{:S(2)}, u32[]{:S(2)}) async-start(bf16[32,1,40,128]{3,2,1,0:T(8,128)(2,1)} %broadcast_in_dim.38), calls=%async_computation | async-start | bytes 655360 | tf_op jit(solution)/shard_map/all_to_all | solution.py:217
  10.1 12.0 %all-to-all-done = bf16[32,1,40,128]{3,2,1,0:T(8,128)(2,1)S(1)} async-done(((bf16[32,1,40,128]{3,2,1,0:T(8,128)(2,1)}), bf16[32,1,40,128]{3,2,1,0:T(8,128)(2,1)S(1)}, u32[]{:S(2)}, u32[]{:S(2)}) %all-to-all-start) | async-done | bytes 327712 | tf_op jit(solution)/shard_map/all_to_all | solution.py:217
  22.2 0.0 copy-start
  22.2 1.2 %copy-done = bf16[4,1024,128]{2,1,0:T(8,128)(2,1)S(1)} copy-done((bf16[4,1024,128]{2,1,0:T(8,128)(2,1)S(1)}, bf16[4,1024,128]{2,1,0:T(8,128)(2,1)}, u32[]{:S(2)}) %copy-start) | copy-done | bytes 1048600
  23.4 11.3 %pairs.1 = (bf16[32,32,128]{2,1,0:T(8,128)(2,1)S(1)}, f32[4,1024,128]{2,1,0:T(8,128)}) custom-call(s32[1]{0:T(128)} %bitcast.first_ref, bf16[32,40,128]{2,1,0:T(8,128)(2,1)S(1)} %bitcast.15, bf16[4,1024,128]{2,1,0:T(8,128)(2,1)S(1)} %copy-done), custom_call_target="tpu_custom_call" | custom-call | tf_op jit(solution)/shard_map/pairs/pallas_call | solution.py:178
  34.7 12.1 %all_to_all.10 = bf16[32,1,32,128]{3,2,1,0:T(8,128)(2,1)S(1)} all-to-all(bf16[32,1,32,128]{3,2,1,0:T(8,128)(2,1)S(1)} %bitcast.16), channel_id=1, replica_groups=mesh['dp'=4,'inner'=8] {'dp','inner'}, dimensions={0} | all-to-all | bytes 524288 | tf_op jit(solution)/shard_map/all_to_all | solution.py:219
  46.7 0.7 %convert_reduce_fusion = f32[32,128]{1,0:T(8,128)} fusion(bf16[32,1,32,128]{3,2,1,0:T(8,128)(2,1)S(1)} %all_to_all.10), kind=kLoop, calls=%fused_computation | loop fusion | flops 258048 | bytes 278528 | tf_op jit(solution)/shard_map/reduce_sum | solution.py:220
  (2 shorter events, 0.0 us)
Async XLA Ops:
  2.8 19.4 %all-to-all-start = ((bf16[32,1,40,128]{3,2,1,0:T(8,128)(2,1)}), bf16[32,1,40,128]{3,2,1,0:T(8,128)(2,1)S(1)}, u32[]{:S(2)}, u32[]{:S(2)}) async-start(bf16[32,1,40,128]{3,2,1,0:T(8,128)(2,1)} %broadcast_in_dim.38), calls=%async_computation | async-start | bytes 655360 | tf_op jit(solution)/shard_map/all_to_all | solution.py:217
  22.2 1.2 %copy-start = (bf16[4,1024,128]{2,1,0:T(8,128)(2,1)S(1)}, bf16[4,1024,128]{2,1,0:T(8,128)(2,1)}, u32[]{:S(2)}) copy-start(bf16[4,1024,128]{2,1,0:T(8,128)(2,1)} %pages_ref.1) | copy-start | bytes 3145732
